TPU v7x, 32 devices: a whole 2x2x4 slice. The times are simulated.
32 devices in a mesh: slab: 4 (over z), xsec: 8 (over y, x, core).
Axes of the slice: x: 2, y: 2, z: 4, core: 2. Of those that a mesh axis runs over, the one named last changes fastest.
Arguments:
- phases: float32 [128, 16, 256], P(('slab', 'xsec')), may hold values from -3.140625 to 3.140625
- onsite: bfloat16 [128, 256, 256], P(('slab', 'xsec')), may hold values from -0.375 to 0.375
- coupling: bfloat16 [128, 256, 256], P(('slab', 'xsec')), may hold values from -0.375 to 0.375
- pair_blocks: bfloat16 [768, 256, 256], P(('slab', 'xsec')), may hold values from -0.375 to 0.375
- pair_source: int32 [768], P(('slab', 'xsec')), may hold values from 0 to 3
- pair_partner: int32 [768], P(('slab', 'xsec')), may hold values from 0 to 31, as said below
Outputs:
- first: float32 [128, 16, 256], P(('slab', 'xsec'))
- second: float32 [128, 16, 256], P(('slab', 'xsec'))
Inputs may be any that keep to these rules, and one draw needn't show every extreme that they name: `pair_partner`: the stored blocks of one device name at most 6 partner clusters on any one device of the slab, and exactly 6 on some device.
All inputs are finite; a program needn't handle non-finite values.
Results may differ from a plain program's by a relative error of at most 0.0043.
Values may be sent and summed in bfloat16 or wider, within the bound.
A program may use at most 64 MiB of HBM per device.

v0:
```python
import math

import jax
import jax.numpy as jnp
from jax import lax
from jax.sharding import PartitionSpec as P


def passed_along(value, axis, steps):
    count = lax.axis_size(axis)
    first, last = (max(0, -steps), min(count, count - steps))
    return lax.ppermute(value, axis, [(source, source + steps) for source in range(first, last)])


def per_device(phases, onsite, coupling, pair_blocks, pair_source, pair_partner):
    clusters = onsite.shape[0]
    pair_count = pair_blocks.shape[0]
    devices_x = lax.axis_size("xsec")
    capacity = max(2, (2 * pair_count + devices_x - 1) // devices_x)
    slot_total = devices_x * capacity
    factor = 1.0 / math.sqrt(3.0 + 2.0 * pair_count / clusters)
    highest = lax.Precision.HIGHEST
    pair_range = jnp.arange(pair_count, dtype=jnp.int32)
    target_device = pair_partner // clusters
    target_slot = pair_partner % clusters
    before = (target_device[None, :] == target_device[:, None]) & (
        pair_range[None, :] < pair_range[:, None]
    )
    ranking = jnp.sum(before.astype(jnp.int32), axis=1)
    position = target_device * capacity + ranking
    pair_table = position[:, None] == jnp.arange(slot_total, dtype=jnp.int32)[None, :]
    request = jnp.sum(jnp.where(pair_table, target_slot[:, None], 0), axis=0).reshape(
        devices_x, capacity
    )
    filled = jnp.any(pair_table, axis=0).astype(jnp.int32).reshape(devices_x, capacity)
    wanted, wanted_live = (
        lax.all_to_all(request, "xsec", split_axis=0, concat_axis=0, tiled=True),
        lax.all_to_all(filled, "xsec", split_axis=0, concat_axis=0, tiled=True),
    )
    cluster_range = jnp.arange(clusters, dtype=jnp.int32)
    want_table = (wanted.reshape(-1)[:, None] == cluster_range[None, :]) & (
        wanted_live.reshape(-1)[:, None] == 1
    )
    source_table = pair_source[:, None] == cluster_range[None, :]
    want_bf = want_table.astype(jnp.bfloat16)
    want_f32 = want_table.astype(jnp.float32)
    pair_bf = pair_table.astype(jnp.bfloat16)
    pair_f32 = pair_table.astype(jnp.float32)
    source_bf = source_table.astype(jnp.bfloat16)
    source_f32 = source_table.astype(jnp.float32)

    def apply_field(field):
        result = 0.5 * (
            jnp.einsum("cij,cpj->cpi", onsite, field, preferred_element_type=jnp.float32)
            + jnp.einsum("cji,cpj->cpi", onsite, field, preferred_element_type=jnp.float32)
        )
        upper = passed_along(field, "slab", -1)
        result = result + jnp.einsum(
            "cij,cpj->cpi", coupling, upper, preferred_element_type=jnp.float32
        )
        downward = jnp.einsum("cji,cpj->cpi", coupling, field, preferred_element_type=jnp.float32)
        result = result + passed_along(downward, "slab", 1)
        outgoing = jnp.einsum(
            "sc,cpi->spi", want_bf, field, preferred_element_type=jnp.float32
        ).astype(jnp.bfloat16)
        outgoing = outgoing.reshape((devices_x, capacity) + field.shape[1:])
        fetched = lax.all_to_all(outgoing, "xsec", split_axis=0, concat_axis=0, tiled=True).reshape(
            (slot_total,) + field.shape[1:]
        )
        partner_x = jnp.einsum(
            "ks,spi->kpi", pair_bf, fetched, preferred_element_type=jnp.float32
        ).astype(jnp.bfloat16)
        own_x = jnp.einsum(
            "kc,cpi->kpi", source_bf, field, preferred_element_type=jnp.float32
        ).astype(jnp.bfloat16)
        forward = jnp.einsum(
            "kij,kpj->kpi", pair_blocks, partner_x, preferred_element_type=jnp.float32
        )
        backward = jnp.einsum(
            "kji,kpj->kpi", pair_blocks, own_x, preferred_element_type=jnp.float32
        )
        result = result + jnp.einsum("kc,kpi->cpi", source_f32, forward, precision=highest)
        returning = jnp.einsum("ks,kpi->spi", pair_f32, backward, precision=highest)
        returning = returning.reshape((devices_x, capacity) + field.shape[1:])
        arrived = lax.all_to_all(
            returning, "xsec", split_axis=0, concat_axis=0, tiled=True
        ).reshape((slot_total,) + field.shape[1:])
        result = result + jnp.einsum("sc,spi->cpi", want_f32, arrived, precision=highest)
        return result * factor

    start = math.sqrt(2.0) * jnp.cos(phases)
    first = apply_field(start.astype(jnp.bfloat16))
    second = 2.0 * apply_field(first.astype(jnp.bfloat16)) - start
    return (first, second)


def solution(mesh):
    return jax.shard_map(
        per_device,
        mesh=mesh,
        in_specs=(
            P(("slab", "xsec"), None, None),
            P(("slab", "xsec"), None, None),
            P(("slab", "xsec"), None, None),
            P(("slab", "xsec"), None, None),
            P(("slab", "xsec")),
            P(("slab", "xsec")),
        ),
        out_specs=(P(("slab", "xsec"), None, None), P(("slab", "xsec"), None, None)),
        check_vma=False,
    )
```

profile of v0, /device:TPU:0, one launch (start us, length us, event | category | flops | bytes accessed | tf_op | source)
XLA Modules:
  0.0 106.6 jit_solution(818090802837610619)
XLA Ops:
  0.6 0.8 and_select_fusion.1
  1.7 0.7 all_to_all.22
  2.4 5.2 %all-to-all-start = ((s32[8,1,6]{2,1,0:T(1,128)}), s32[8,1,6]{2,1,0:T(1,128)S(1)}, u32[]{:S(2)}, u32[]{:S(2)}) async-start(s32[8,1,6]{2,1,0:T(1,128)} %bitcast.2), calls=%async_computation | async-start | bytes 8192 | tf_op jit(solution)/shard_map/all_to_all | solution.py:37
  7.6 1.7 %fusion.33 = bf16[4,16,256]{2,1,0:T(8,128)(2,1)} fusion(f32[4,16,256]{2,1,0:T(8,128)} %param.6), kind=kLoop, calls=%fused_computation.44 | loop fusion | flops 32768 | bytes 98304 | tf_op jit(solution)/shard_map/convert_element_type | solution.py:92
  9.3 1.3 %collective-permute-start = (bf16[4,16,256]{2,1,0:T(8,128)(2,1)}, bf16[4,16,256]{2,1,0:T(8,128)(2,1)}, u32[]{:S(2)}, u32[]{:S(2)}) collective-permute-start(bf16[4,16,256]{2,1,0:T(8,128)(2,1)} %fusion.33), channel_id=1, source_target_pairs={{8,0},{16,8},{24,16},{9,1},{17,9},{25,17},{10,2},{18,10},{26,18},{... | collective-permute-start | bytes 98312 | tf_op jit(solution)/shard_map/ppermute | solution.py:12
  10.6 1.9 %fusion.58 = f32[4,16,256]{2,1,0:T(8,128)} fusion(bf16[4,16,256]{2,1,0:T(8,128)(2,1)} %fusion.33, bf16[4,256,256]{2,1,0:T(8,128)(2,1)} %param.8), kind=kOutput, calls=%fused_computation.74 | convolution fusion | flops 8388608 | bytes 622592 | tf_op jit(solution)/shard_map/cji,cpj->cpi/dot_general | solution.py:61
  12.4 5.2 %collective-permute-start.1 = (f32[4,16,256]{2,1,0:T(8,128)}, f32[4,16,256]{2,1,0:T(8,128)}, u32[]{:S(2)}, u32[]{:S(2)}) collective-permute-start(f32[4,16,256]{2,1,0:T(8,128)} %fusion.58), channel_id=1, source_target_pairs={{0,8},{8,16},{16,24},{1,9},{9,17},{17,25},{2,10},{10,18},{18,26},{... | collective-permute-start | bytes 196616 | tf_op jit(solution)/shard_map/ppermute | solution.py:12
  17.6 1.0 convolution_convert_fusion.3
  18.7 0.5 fusion.29
  19.2 1.6 %fusion.20 = f32[48,16,256]{2,0,1:T(8,128)} fusion(f32[24,16,256]{2,1,0:T(8,128)S(1)} %fusion.29, s32[24]{0:T(128)S(1)} %multiply_add_fusion), kind=kOutput, calls=%fused_computation.30 | convolution fusion | flops 56624256 | bytes 1179744 | tf_op jit(solution)/shard_map/ks,kpi->spi/dot_general | solution.py:83
  20.9 0.7 reshape.73
  21.6 4.2 %all-to-all-start.1 = ((s32[8,1,6]{2,1,0:T(1,128)}), s32[8,1,6]{2,1,0:T(1,128)S(1)}, u32[]{:S(2)}, u32[]{:S(2)}) async-start(s32[8,1,6]{2,1,0:T(1,128)} %bitcast.3), calls=%async_computation.1 | async-start | bytes 8192 | tf_op jit(solution)/shard_map/all_to_all | solution.py:38
  25.8 0.5 broadcast.65
  26.3 0.7 reduce.5
  27.0 3.4 %all-to-all-done.1 = s32[8,1,6]{2,1,0:T(1,128)S(1)} async-done(((s32[8,1,6]{2,1,0:T(1,128)}), s32[8,1,6]{2,1,0:T(1,128)S(1)}, u32[]{:S(2)}, u32[]{:S(2)}) %all-to-all-start.1) | async-done | bytes 224 | tf_op jit(solution)/shard_map/all_to_all | solution.py:38
  30.6 1.1 %convolution_convert_fusion.1 = bf16[48,16,256]{2,0,1:T(8,128)(2,1)S(1)} fusion(pred[48,4,1]{0,1,2:T(4,128)(4,1)S(1)} %fusion.51, bf16[4,16,256]{2,1,0:T(8,128)(2,1)} %fusion.33), kind=kOutput, calls=%fused_computation.1 | convolution fusion | flops 1769472 | bytes 426176 | tf_op jit(solution)/shard_map/sc,cpi->spi/dot_general | solution.py:63
  31.7 0.9 copy.81
  32.5 3.5 %all-to-all-start.2 = ((bf16[8,6,16,256]{3,2,1,0:T(8,128)(2,1)}), bf16[8,6,16,256]{3,2,1,0:T(8,128)(2,1)S(1)}, u32[]{:S(2)}, u32[]{:S(2)}) async-start(bf16[8,6,16,256]{3,2,1,0:T(8,128)(2,1)} %bitcast.5), calls=%async_computation.2 | async-start | bytes 786432 | tf_op jit(solution)/shard_map/all_to_all | solution.py:67
  36.0 1.3 %fusion.57 = f32[4,16,256]{2,1,0:T(8,128)S(1)} fusion(bf16[4,16,256]{2,1,0:T(8,128)(2,1)} %fusion.33, bf16[4,256,256]{2,1,0:T(8,128)(2,1)} %param.7), kind=kOutput, calls=%fused_computation.73 | convolution fusion | flops 8388608 | bytes 622592 | tf_op jit(solution)/shard_map/cij,cpj->cpi/dot_general | solution.py:54
  37.3 2.5 %copy.89 = f32[48,16,256]{2,1,0:T(8,128)} copy(f32[48,16,256]{2,0,1:T(8,128)} %fusion.20) | data formatting | bytes 1572864 | tf_op jit(solution)/shard_map/ks,kpi->spi/dot_general | solution.py:83
  39.8 1.9 %fusion = f32[4,16,256]{2,1,0:T(8,128)} fusion(f32[4,16,256]{2,1,0:T(8,128)S(1)} %fusion.57, bf16[4,16,256]{2,1,0:T(8,128)(2,1)} %fusion.33, bf16[4,256,256]{2,1,0:T(8,128)(2,1)} %param.7), kind=kOutput, calls=%fused_computation.10 | convolution fusion | flops 8421376 | bytes 688128 | tf_op jit(solution)/shard_map/cji,cpj->cpi/dot_general | solution.py:55
  41.7 2.6 %all-to-all-done.2 = bf16[8,6,16,256]{3,2,1,0:T(8,128)(2,1)S(1)} async-done(((bf16[8,6,16,256]{3,2,1,0:T(8,128)(2,1)}), bf16[8,6,16,256]{3,2,1,0:T(8,128)(2,1)S(1)}, u32[]{:S(2)}, u32[]{:S(2)}) %all-to-all-start.2) | async-done | bytes 393248 | tf_op jit(solution)/shard_map/all_to_all | solution.py:67
  44.3 4.2 %all-to-all-start.3 = ((f32[8,6,16,256]{3,2,1,0:T(8,128)}), f32[8,6,16,256]{3,2,1,0:T(8,128)}, u32[]{:S(2)}, u32[]{:S(2)}) async-start(f32[8,6,16,256]{3,2,1,0:T(8,128)} %bitcast.49), calls=%async_computation.3 | async-start | bytes 1572864 | tf_op jit(solution)/shard_map/all_to_all | solution.py:85
  48.7 0.9 fusion.31
  49.7 0.5 fusion.22
  50.2 10.9 %all-to-all-done.3 = f32[8,6,16,256]{3,2,1,0:T(8,128)} async-done(((f32[8,6,16,256]{3,2,1,0:T(8,128)}), f32[8,6,16,256]{3,2,1,0:T(8,128)}, u32[]{:S(2)}, u32[]{:S(2)}) %all-to-all-start.3) | async-done | bytes 786464 | tf_op jit(solution)/shard_map/all_to_all | solution.py:85
  61.1 2.0 %fusion.13 = f32[4,16,256]{2,0,1:T(4,128)S(1)} fusion(pred[48,4,1]{0,1,2:T(4,128)(4,1)S(1)} %fusion.51, f32[48,16,256]{2,1,0:T(8,128)} %bitcast.8), kind=kOutput, calls=%fused_computation.23 | convolution fusion | flops 9437184 | bytes 852160 | tf_op jit(solution)/shard_map/sc,spi->cpi/dot_general | solution.py:88
  63.1 1.9 %fusion.56 = (bf16[4,16,256]{2,1,0:T(8,128)(2,1)}, f32[4,16,256]{2,1,0:T(8,128)}) fusion(f32[4,16,256]{2,0,1:T(4,128)S(1)} %fusion.13, f32[4,16,256]{2,0,1:T(4,128)S(1)} %fusion.22, f32[4,16,256]{2,1,0:T(8,128)} %collective-permute-done.1, f32[4,16,256]{2,1,0:T(8,128)S(1)} %copy-done.2, bf16[4,16,256]{2,1,0:T(8,128)(2,1)} %collective-permute-done, ...), kind=kOutput, calls=%fused_computation.72 | convolution fusion | flops 8486912 | bytes 917504 | tf_op jit(solution)/shard_map/cij,cpj->cpi/dot_general | solution.py:58
  65.0 1.0 convolution_convert_fusion.2
  66.0 1.1 %convolution_convert_fusion = bf16[48,16,256]{2,0,1:T(8,128)(2,1)S(1)} fusion(pred[48,4,1]{0,1,2:T(4,128)(4,1)S(1)} %fusion.51, bf16[4,16,256]{2,1,0:T(8,128)(2,1)} %get-tuple-element.4), kind=kOutput, calls=%fused_computation | convolution fusion | flops 1769472 | bytes 426176 | tf_op jit(solution)/shard_map/sc,cpi->spi/dot_general | solution.py:63
  67.1 1.9 %fusion.59 = f32[4,16,256]{2,1,0:T(8,128)} fusion(bf16[4,16,256]{2,1,0:T(8,128)(2,1)} %get-tuple-element.4, bf16[4,256,256]{2,1,0:T(8,128)(2,1)} %param.7), kind=kOutput, calls=%fused_computation.75 | convolution fusion | flops 8388608 | bytes 622592 | tf_op jit(solution)/shard_map/cij,cpj->cpi/dot_general | solution.py:54
  69.1 1.6 %fusion.60 = f32[4,16,256]{2,1,0:T(8,128)} fusion(bf16[4,16,256]{2,1,0:T(8,128)(2,1)} %get-tuple-element.4, bf16[4,256,256]{2,1,0:T(8,128)(2,1)S(1)} %copy-done.1), kind=kOutput, calls=%fused_computation.76 | convolution fusion | flops 8388608 | bytes 622592 | tf_op jit(solution)/shard_map/cji,cpj->cpi/dot_general | solution.py:61
  70.6 1.3 %collective-permute-start.2 = (bf16[4,16,256]{2,1,0:T(8,128)(2,1)}, bf16[4,16,256]{2,1,0:T(8,128)(2,1)}, u32[]{:S(2)}, u32[]{:S(2)}) collective-permute-start(bf16[4,16,256]{2,1,0:T(8,128)(2,1)} %get-tuple-element.4), channel_id=1, source_target_pairs={{8,0},{16,8},{24,16},{9,1},{17,9},{25,17},{10,2},{18,10},{26,18},{... | collective-permute-start | bytes 98312 | tf_op jit(solution)/shard_map/ppermute | solution.py:12
  71.9 0.5 fusion.25
  72.4 0.9 copy.93
  73.3 4.1 %all-to-all-start.4 = ((bf16[8,6,16,256]{3,2,1,0:T(8,128)(2,1)}), bf16[8,6,16,256]{3,2,1,0:T(8,128)(2,1)}, u32[]{:S(2)}, u32[]{:S(2)}) async-start(bf16[8,6,16,256]{3,2,1,0:T(8,128)(2,1)} %bitcast.9), calls=%async_computation.4 | async-start | bytes 786432 | tf_op jit(solution)/shard_map/all_to_all | solution.py:67
  77.4 0.7 fusion.15
  78.2 1.3 %copy.101 = f32[48,16,256]{2,1,0:T(8,128)} copy(f32[48,16,256]{2,0,1:T(8,128)S(1)} %fusion.15) | data formatting | bytes 1572864 | tf_op jit(solution)/shard_map/ks,kpi->spi/dot_general | solution.py:83
  79.5 4.6 %collective-permute-start.3 = (f32[4,16,256]{2,1,0:T(8,128)}, f32[4,16,256]{2,1,0:T(8,128)S(1)}, u32[]{:S(2)}, u32[]{:S(2)}) collective-permute-start(f32[4,16,256]{2,1,0:T(8,128)} %fusion.60), channel_id=1, source_target_pairs={{0,8},{8,16},{16,24},{1,9},{9,17},{17,25},{2,10},{10,18},{18,26},{... | collective-permute-start | bytes 196616 | tf_op jit(solution)/shard_map/ppermute | solution.py:12
  84.1 1.2 %fusion.5 = f32[4,16,256]{2,1,0:T(8,128)S(1)} fusion(f32[4,16,256]{2,1,0:T(8,128)} %fusion.59, bf16[4,16,256]{2,1,0:T(8,128)(2,1)} %get-tuple-element.4, bf16[4,256,256]{2,1,0:T(8,128)(2,1)} %param.7), kind=kOutput, calls=%fused_computation.15 | convolution fusion | flops 8421376 | bytes 688128 | tf_op jit(solution)/shard_map/cji,cpj->cpi/dot_general | solution.py:55
  85.3 0.5 all-to-all-done.4
  85.8 4.2 %all-to-all-start.5 = ((f32[8,6,16,256]{3,2,1,0:T(8,128)}), f32[8,6,16,256]{3,2,1,0:T(8,128)}, u32[]{:S(2)}, u32[]{:S(2)}) async-start(f32[8,6,16,256]{3,2,1,0:T(8,128)} %bitcast.48), calls=%async_computation.5 | async-start | bytes 1572864 | tf_op jit(solution)/shard_map/all_to_all | solution.py:85
  90.0 1.3 %convolution_convert_fusion.4 = bf16[24,16,256]{2,0,1:T(8,128)(2,1)S(1)} fusion(bf16[48,16,256]{2,1,0:T(8,128)(2,1)} %bitcast.10, s32[24]{0:T(128)S(1)} %multiply_add_fusion), kind=kOutput, calls=%fused_computation.4 | convolution fusion | flops 9536640 | bytes 589920 | tf_op jit(solution)/shard_map/ks,spi->kpi/dot_general | solution.py:70
  91.3 0.9 fusion.27
  92.2 0.5 fusion.17
  92.7 9.9 %all-to-all-done.5 = f32[8,6,16,256]{3,2,1,0:T(8,128)} async-done(((f32[8,6,16,256]{3,2,1,0:T(8,128)}), f32[8,6,16,256]{3,2,1,0:T(8,128)}, u32[]{:S(2)}, u32[]{:S(2)}) %all-to-all-start.5) | async-done | bytes 786464 | tf_op jit(solution)/shard_map/all_to_all | solution.py:85
  102.6 1.9 %fusion.11 = f32[4,16,256]{2,0,1:T(4,128)S(1)} fusion(pred[48,4,1]{0,1,2:T(4,128)(4,1)S(1)} %fusion.51, f32[48,16,256]{2,1,0:T(8,128)} %bitcast.12), kind=kOutput, calls=%fused_computation.21 | convolution fusion | flops 9437184 | bytes 852160 | tf_op jit(solution)/shard_map/sc,spi->cpi/dot_general | solution.py:88
  104.5 2.0 %fusion.10 = f32[4,16,256]{2,1,0:T(8,128)} fusion(f32[4,16,256]{2,1,0:T(8,128)S(1)} %collective-permute-done.3, f32[4,16,256]{2,1,0:T(8,128)S(1)} %fusion.5, bf16[4,16,256]{2,1,0:T(8,128)(2,1)} %collective-permute-done.2, bf16[4,256,256]{2,1,0:T(8,128)(2,1)} %param.8, f32[4,16,256]{2,0,1:T(4,128)S(1)} %fusion.11, f32[4,16,256]{2,0,1:T(4,128)S(1)} %fusion.17, ...), kind=kOutput, calls=%fused_computation.20 | convolution fusion | flops 8503296 | bytes 950272 | tf_op jit(solution)/shard_map/cij,cpj->cpi/dot_general | solution.py:58
  (25 shorter events, 0.9 us)
Async XLA Ops:
  0.6 18.0 %copy-start = (bf16[24,256,256]{2,1,0:T(8,128)(2,1)S(1)}, bf16[24,256,256]{2,1,0:T(8,128)(2,1)}, u32[]{:S(2)}) copy-start(bf16[24,256,256]{2,1,0:T(8,128)(2,1)} %param.9) | copy-start | bytes 9437188
  2.4 19.1 %all-to-all-start = ((s32[8,1,6]{2,1,0:T(1,128)}), s32[8,1,6]{2,1,0:T(1,128)S(1)}, u32[]{:S(2)}, u32[]{:S(2)}) async-start(s32[8,1,6]{2,1,0:T(1,128)} %bitcast.2), calls=%async_computation | async-start | bytes 8192 | tf_op jit(solution)/shard_map/all_to_all | solution.py:37
  9.3 53.8 %collective-permute-start = (bf16[4,16,256]{2,1,0:T(8,128)(2,1)}, bf16[4,16,256]{2,1,0:T(8,128)(2,1)}, u32[]{:S(2)}, u32[]{:S(2)}) collective-permute-start(bf16[4,16,256]{2,1,0:T(8,128)(2,1)} %fusion.33), channel_id=1, source_target_pairs={{8,0},{16,8},{24,16},{9,1},{17,9},{25,17},{10,2},{18,10},{26,18},{... | collective-permute-start | bytes 98312 | tf_op jit(solution)/shard_map/ppermute | solution.py:12
  12.4 50.6 %collective-permute-start.1 = (f32[4,16,256]{2,1,0:T(8,128)}, f32[4,16,256]{2,1,0:T(8,128)}, u32[]{:S(2)}, u32[]{:S(2)}) collective-permute-start(f32[4,16,256]{2,1,0:T(8,128)} %fusion.58), channel_id=1, source_target_pairs={{0,8},{8,16},{16,24},{1,9},{9,17},{17,25},{2,10},{10,18},{18,26},{... | collective-permute-start | bytes 196616 | tf_op jit(solution)/shard_map/ppermute | solution.py:12
  21.6 8.9 %all-to-all-start.1 = ((s32[8,1,6]{2,1,0:T(1,128)}), s32[8,1,6]{2,1,0:T(1,128)S(1)}, u32[]{:S(2)}, u32[]{:S(2)}) async-start(s32[8,1,6]{2,1,0:T(1,128)} %bitcast.3), calls=%async_computation.1 | async-start | bytes 8192 | tf_op jit(solution)/shard_map/all_to_all | solution.py:38
  32.5 11.7 %all-to-all-start.2 = ((bf16[8,6,16,256]{3,2,1,0:T(8,128)(2,1)}), bf16[8,6,16,256]{3,2,1,0:T(8,128)(2,1)S(1)}, u32[]{:S(2)}, u32[]{:S(2)}) async-start(bf16[8,6,16,256]{3,2,1,0:T(8,128)(2,1)} %bitcast.5), calls=%async_computation.2 | async-start | bytes 786432 | tf_op jit(solution)/shard_map/all_to_all | solution.py:67
  39.8 9.9 %copy-start.4 = (s32[24]{0:T(128)S(1)}, s32[24]{0:T(128)}, u32[]{:S(2)}) copy-start(s32[24]{0:T(128)} %param.10) | copy-start | bytes 292
  44.3 16.8 %all-to-all-start.3 = ((f32[8,6,16,256]{3,2,1,0:T(8,128)}), f32[8,6,16,256]{3,2,1,0:T(8,128)}, u32[]{:S(2)}, u32[]{:S(2)}) async-start(f32[8,6,16,256]{3,2,1,0:T(8,128)} %bitcast.49), calls=%async_computation.3 | async-start | bytes 1572864 | tf_op jit(solution)/shard_map/all_to_all | solution.py:85
  48.7 14.3 %copy-start.2 = (f32[4,16,256]{2,1,0:T(8,128)S(1)}, f32[4,16,256]{2,1,0:T(8,128)}, u32[]{:S(2)}) copy-start(f32[4,16,256]{2,1,0:T(8,128)} %fusion) | copy-start | bytes 196612
  61.1 8.0 %copy-start.1 = (bf16[4,256,256]{2,1,0:T(8,128)(2,1)S(1)}, bf16[4,256,256]{2,1,0:T(8,128)(2,1)}, u32[]{:S(2)}) copy-start(bf16[4,256,256]{2,1,0:T(8,128)(2,1)} %param.8) | copy-start | bytes 1572868
  70.6 33.9 %collective-permute-start.2 = (bf16[4,16,256]{2,1,0:T(8,128)(2,1)}, bf16[4,16,256]{2,1,0:T(8,128)(2,1)}, u32[]{:S(2)}, u32[]{:S(2)}) collective-permute-start(bf16[4,16,256]{2,1,0:T(8,128)(2,1)} %get-tuple-element.4), channel_id=1, source_target_pairs={{8,0},{16,8},{24,16},{9,1},{17,9},{25,17},{10,2},{18,10},{26,18},{... | collective-permute-start | bytes 98312 | tf_op jit(solution)/shard_map/ppermute | solution.py:12
  73.3 12.5 %all-to-all-start.4 = ((bf16[8,6,16,256]{3,2,1,0:T(8,128)(2,1)}), bf16[8,6,16,256]{3,2,1,0:T(8,128)(2,1)}, u32[]{:S(2)}, u32[]{:S(2)}) async-start(bf16[8,6,16,256]{3,2,1,0:T(8,128)(2,1)} %bitcast.9), calls=%async_computation.4 | async-start | bytes 786432 | tf_op jit(solution)/shard_map/all_to_all | solution.py:67
  79.5 25.0 %collective-permute-start.3 = (f32[4,16,256]{2,1,0:T(8,128)}, f32[4,16,256]{2,1,0:T(8,128)S(1)}, u32[]{:S(2)}, u32[]{:S(2)}) collective-permute-start(f32[4,16,256]{2,1,0:T(8,128)} %fusion.60), channel_id=1, source_target_pairs={{0,8},{8,16},{16,24},{1,9},{9,17},{17,25},{2,10},{10,18},{18,26},{... | collective-permute-start | bytes 196616 | tf_op jit(solution)/shard_map/ppermute | solution.py:12
  85.8 16.8 %all-to-all-start.5 = ((f32[8,6,16,256]{3,2,1,0:T(8,128)}), f32[8,6,16,256]{3,2,1,0:T(8,128)}, u32[]{:S(2)}, u32[]{:S(2)}) async-start(f32[8,6,16,256]{3,2,1,0:T(8,128)} %bitcast.48), calls=%async_computation.5 | async-start | bytes 1572864 | tf_op jit(solution)/shard_map/all_to_all | solution.py:85
  90.0 14.5 %copy-start.3 = (f32[4,16,256]{2,1,0:T(8,128)S(1)}, f32[4,16,256]{2,1,0:T(8,128)}, u32[]{:S(2)}) copy-start(f32[4,16,256]{2,1,0:T(8,128)} %param.6) | copy-start | bytes 196612
where the time goes:
time: 108 us; the launch traced here: 107 us
  starting transfers between devices  37.6 us (35%)
  matrix products  29.5 us (27%)
  waiting for transfers between devices  27.3 us (25%)
  local copies, waits for them, and re-layouts  7.67 us (7%)
  other arithmetic  3.57 us (3%)
    all_to_all x2, waiting for transfers between devices, apply_field(): lax.all_to_all(returning, 'xsec', split_axis=0, concat_axis=0, tiled=True)  20.8 us
    ppermute x4, starting transfers between devices, passed_along(): lax.ppermute(value, axis, [(source, source + steps) for source in range(f...  12.3 us
    all_to_all x2, starting transfers between devices, apply_field(): lax.all_to_all(returning, 'xsec', split_axis=0, concat_axis=0, tiled=True)  8.43 us
    all_to_all x2, starting transfers between devices, apply_field(): lax.all_to_all(outgoing, 'xsec', split_axis=0, concat_axis=0, tiled=True)  7.54 us
    all_to_all x1, starting transfers between devices, per_device(): lax.all_to_all(request, 'xsec', split_axis=0, concat_axis=0, tiled=True)  5.17 us
    all_to_all x1, starting transfers between devices, per_device(): lax.all_to_all(filled, 'xsec', split_axis=0, concat_axis=0, tiled=True)  4.2 us
    dot_general x2, matrix products, apply_field(): jnp.einsum('cij,cpj->cpi', coupling, upper, preferred_element_type=jnp.fl...  3.96 us
    dot_general x2, local copies, waits for them, and re-layouts, apply_field(): returning = jnp.einsum('ks,kpi->spi', pair_f32, backward, precision=highest)  3.86 us
  transfers between devices with their start and end apart: 10, of which 5 were waited for; matrix products, arithmetic and copies ran while one was open for 28% of the time, Pallas kernels for 0%

commit v1 on v0

v1 whole, which is shorter than its diff:
```python
import functools
import math

import jax
import jax.numpy as jnp
from jax import lax
from jax.experimental import pallas as pl
from jax.experimental.pallas import tpu as pltpu
from jax.sharding import PartitionSpec as P

F32 = jnp.float32
BF16 = jnp.bfloat16
CHUNKS = 4


def cosine(x):
    h = 0.5 * x
    square = h * h
    total = jnp.full_like(square, 1.0 / math.factorial(13))
    for order in (11, 9, 7, 5, 3, 1):
        sign = 1.0 if order % 4 == 1 else -1.0
        total = total * square + sign / math.factorial(order)
    sine = h * total
    return 1.0 - 2.0 * sine * sine


def plain(left, right):
    return lax.dot_general(left, right, (((1,), (0,)), ((), ())), preferred_element_type=F32)


def flipped(left, right):
    return lax.dot_general(left, right, (((1,), (1,)), ((), ())), preferred_element_type=F32)


def halves(value):
    high = value.astype(BF16)
    return high, (value - high.astype(F32)).astype(BF16)


def kernel(
    slabs, peers, clusters, pairs, probes, orb,
    partner_ref, source_ref, phases_hbm, onsite_hbm, coupling_hbm, pairs_hbm,
    first_ref, second_ref,
    onsite, coupling, blocks, phases, start, fields_0, fields_1, own, above, going, coming, down_out, down_in,
    spread, collect, products_high, products_low,
    load_sem, field_send, field_recv, prod_send, prod_recv, up_send, up_recv, down_send, down_recv,
):
    slab = lax.axis_index("slab")
    me = lax.axis_index("xsec")
    rows = clusters * probes
    factor = 1.0 / math.sqrt(3.0 + 2.0 * pairs / clusters)
    part = pairs // CHUNKS
    fields = (fields_0, fields_1)

    loads = [
        pltpu.make_async_copy(phases_hbm, phases, load_sem.at[2 + CHUNKS]),
        pltpu.make_async_copy(coupling_hbm, coupling, load_sem.at[0]),
    ]
    for chunk in range(CHUNKS):
        span = pl.ds(chunk * part, part)
        loads.append(
            pltpu.make_async_copy(pairs_hbm.at[span], blocks.at[span], load_sem.at[1 + chunk])
        )
    loads.append(pltpu.make_async_copy(onsite_hbm, onsite, load_sem.at[1 + CHUNKS]))
    for load in loads:
        load.start()
    phases_load, loads = loads[0], loads[1:]

    def peer(offset):
        return lax.rem(me + offset, peers)

    barrier = pltpu.get_barrier_semaphore()
    for offset in range(1, peers):
        pl.semaphore_signal(
            barrier, inc=1, device_id=(slab, peer(offset)), device_id_type=pl.DeviceIdType.MESH
        )

    @pl.when(slab > 0)
    def _():
        pl.semaphore_signal(
            barrier, inc=1, device_id=(slab - 1, me), device_id_type=pl.DeviceIdType.MESH
        )

    @pl.when(slab < slabs - 1)
    def _():
        pl.semaphore_signal(
            barrier, inc=1, device_id=(slab + 1, me), device_id_type=pl.DeviceIdType.MESH
        )

    phases_load.wait()
    begin = math.sqrt(2.0) * cosine(phases[...]).reshape(rows, orb)
    start[...] = begin

    width = pairs * probes
    lane = lax.broadcasted_iota(jnp.int32, (1, width), 1)
    group = lane // probes
    inner = lane % probes
    partner_row = jnp.zeros((1, width), jnp.int32)
    source_row = jnp.zeros((1, width), jnp.int32)
    for k in range(pairs):
        partner_row = jnp.where(group == k, partner_ref[k], partner_row)
        source_row = jnp.where(group == k, source_ref[k], source_row)
    partner_row = partner_row * probes + inner
    source_row = source_row * probes + inner

    neighbours = (slab > 0).astype(jnp.int32) + (slab < slabs - 1).astype(jnp.int32)
    pl.semaphore_wait(barrier, peers - 1 + neighbours)

    def field_copy(step, offset):
        span = fields[step].at[pl.ds(me * clusters, clusters)]
        return pltpu.make_async_remote_copy(
            src_ref=span, dst_ref=span,
            send_sem=field_send.at[step, offset], recv_sem=field_recv.at[step, offset],
            device_id=(slab, peer(offset)), device_id_type=pl.DeviceIdType.MESH,
        )

    def product_copy(step, offset):
        return pltpu.make_async_remote_copy(
            src_ref=going.at[step, pl.ds(peer(offset) * rows, rows)],
            dst_ref=coming.at[step, offset],
            send_sem=prod_send.at[step, offset], recv_sem=prod_recv.at[step, offset],
            device_id=(slab, peer(offset)), device_id_type=pl.DeviceIdType.MESH,
        )

    def up_copy(step):
        return pltpu.make_async_remote_copy(
            src_ref=own.at[step], dst_ref=above.at[step],
            send_sem=up_send.at[step], recv_sem=up_recv.at[step],
            device_id=(slab - 1, me), device_id_type=pl.DeviceIdType.MESH,
        )

    def down_copy(step):
        return pltpu.make_async_remote_copy(
            src_ref=down_out.at[step], dst_ref=down_in.at[step],
            send_sem=down_send.at[step], recv_sem=down_recv.at[step],
            device_id=(slab + 1, me), device_id_type=pl.DeviceIdType.MESH,
        )

    def keep(k, value):
        high, low = halves(value)
        products_high[pl.ds(k * probes, probes)] = high
        products_low[pl.ds(k * probes, probes)] = low

    def apply_field(step, value):
        field = value.astype(BF16).reshape(clusters, probes, orb)
        own[step] = field
        fields[step][pl.ds(me * clusters, clusters)] = field
        for offset in range(1, peers):
            field_copy(step, offset).start()

        @pl.when(slab > 0)
        def _():
            up_copy(step).start()

        if step == 0:
            spread_rows = lax.broadcasted_iota(jnp.int32, spread.shape, 0)
            spread[...] = (spread_rows == partner_row).astype(F32).astype(BF16)
            collect_rows = lax.broadcasted_iota(jnp.int32, collect.shape, 0)
            collect[...] = (collect_rows == source_row).astype(F32).astype(BF16)
            loads[0].wait()
        for c in range(clusters):
            down_out[step, pl.ds(c * probes, probes)] = plain(field[c], coupling[c])

        @pl.when(slab < slabs - 1)
        def _():
            down_copy(step).start()

        for k in range(pairs):
            if step == 0 and k % part == 0:
                loads[1 + k // part].wait()
            keep(k, plain(own[step, source_ref[k]], blocks[k]))
        high = products_high[...]
        low = products_low[...]
        going[step] = (plain(spread[...], high) + plain(spread[...], low)).astype(BF16)
        for offset in range(1, peers):
            product_copy(step, offset).start()

        if step == 0:
            loads[1 + CHUNKS].wait()
        local = []
        for c in range(clusters):
            local.append(0.5 * (plain(field[c], onsite[c]) + flipped(field[c], onsite[c])))
        result = jnp.concatenate(local, axis=0)

        for offset in range(1, peers):
            field_copy(step, offset).wait_recv()
        for k in range(pairs):
            keep(k, flipped(fields[step][partner_ref[k]], blocks[k]))
        high = products_high[...]
        low = products_low[...]
        result = result + (plain(collect[...], high) + plain(collect[...], low))

        @pl.when(slab < slabs - 1)
        def _():
            up_copy(step).wait_recv()

        @pl.when(slab == slabs - 1)
        def _():
            above[step] = jnp.zeros_like(own[step])

        result = result + jnp.concatenate(
            [flipped(above[step, c], coupling[c]) for c in range(clusters)], axis=0
        )

        @pl.when(slab > 0)
        def _():
            down_copy(step).wait_recv()

        @pl.when(slab == 0)
        def _():
            down_in[step] = jnp.zeros_like(start)

        result = result + down_in[step]
        result = result + going[step, pl.ds(me * rows, rows)].astype(F32)
        for offset in range(1, peers):
            product_copy(step, offset).wait_recv()
            result = result + coming[step, offset].astype(F32)
        return result * factor

    first = apply_field(0, begin)
    first_ref[...] = first.reshape(clusters, probes, orb)
    second = 2.0 * apply_field(1, first) - start[...]
    second_ref[...] = second.reshape(clusters, probes, orb)

    for step in range(2):
        for offset in range(1, peers):
            field_copy(step, offset).wait_send()
            product_copy(step, offset).wait_send()

        @pl.when(slab > 0)
        def _():
            up_copy(step).wait_send()

        @pl.when(slab < slabs - 1)
        def _():
            down_copy(step).wait_send()


def per_device(phases, onsite, coupling, pair_blocks, pair_source, pair_partner):
    clusters, probes, orb = phases.shape
    pairs = pair_blocks.shape[0]
    slabs = lax.axis_size("slab")
    peers = lax.axis_size("xsec")
    slots = peers * clusters
    rows = clusters * probes
    vmem = pl.BlockSpec(memory_space=pltpu.VMEM)
    smem = pl.BlockSpec(memory_space=pltpu.SMEM)
    hbm = pl.BlockSpec(memory_space=pltpu.HBM)
    dma = pltpu.SemaphoreType.DMA
    out = jax.ShapeDtypeStruct(phases.shape, F32)
    return pl.pallas_call(
        functools.partial(kernel, slabs, peers, clusters, pairs, probes, orb),
        out_shape=(out, out),
        in_specs=[smem, smem, hbm, hbm, hbm, hbm],
        out_specs=(vmem, vmem),
        scratch_shapes=[
            pltpu.VMEM((clusters, orb, orb), BF16),
            pltpu.VMEM((clusters, orb, orb), BF16),
            pltpu.VMEM((pairs, orb, orb), BF16),
            pltpu.VMEM((clusters, probes, orb), F32),
            pltpu.VMEM((rows, orb), F32),
            pltpu.VMEM((slots, probes, orb), BF16),
            pltpu.VMEM((slots, probes, orb), BF16),
            pltpu.VMEM((2, clusters, probes, orb), BF16),
            pltpu.VMEM((2, clusters, probes, orb), BF16),
            pltpu.VMEM((2, slots * probes, orb), BF16),
            pltpu.VMEM((2, peers, rows, orb), BF16),
            pltpu.VMEM((2, rows, orb), F32),
            pltpu.VMEM((2, rows, orb), F32),
            pltpu.VMEM((slots * probes, pairs * probes), BF16),
            pltpu.VMEM((rows, pairs * probes), BF16),
            pltpu.VMEM((pairs * probes, orb), BF16),
            pltpu.VMEM((pairs * probes, orb), BF16),
            dma((3 + CHUNKS,)),
            dma((2, peers)), dma((2, peers)), dma((2, peers)), dma((2, peers)),
            dma((2,)), dma((2,)), dma((2,)), dma((2,)),
        ],
        compiler_params=pltpu.CompilerParams(
            collective_id=0, has_side_effects=True, vmem_limit_bytes=63 * 1024 * 1024
        ),
    )(pair_partner, pair_source, phases, onsite, coupling, pair_blocks)


def solution(mesh):
    spec = P(("slab", "xsec"), None, None)
    flat = P(("slab", "xsec"))
    return jax.shard_map(
        per_device,
        mesh=mesh,
        in_specs=(spec, spec, spec, spec, flat, flat),
        out_specs=(spec, spec),
        check_vma=False,
    )
```

time: 108 us -> 24.5 us (0.23); the launches traced: 107 us -> 24.3 us
  starting transfers between devices: 37.6 us -> 0 us
  matrix products: 29.5 us -> 0 us
  waiting for transfers between devices: 27.3 us -> 0 us
  Pallas kernels: 0 us -> 20.7 us
  local copies, waits for them, and re-layouts: 7.67 us -> 2.95 us
  other arithmetic: 3.57 us -> 0 us
    dot_general x24 -> x0, matrix products: 29.5 us -> none  [the longest x2 3.96 us: apply_field(): jnp.einsum('cij,cpj->cpi', coupling, upper, preferred_element_type=jnp.fl...]
    all_to_all x6 -> x0, waiting for transfers between devices: 27.3 us -> none  [the longest x2 20.8 us: apply_field(): lax.all_to_all(returning, 'xsec', split_axis=0, concat_axis=0, tiled=True)]
    all_to_all x6 -> x0, starting transfers between devices: 25.4 us -> none  [the longest x2 8.43 us: apply_field(): lax.all_to_all(returning, 'xsec', split_axis=0, concat_axis=0, tiled=True)]
    pallas_call x0 -> x1, Pallas kernels: none -> 20.7 us  [per_device(): pl.pallas_call(functools.partial(kernel, slabs, peers, clusters, pairs, p...]
    ppermute x4 -> x0, starting transfers between devices: 12.3 us -> none  [passed_along(): lax.ppermute(value, axis, [(source, source + steps) for source in range(f...]
    dot_general x2 -> x0, local copies, waits for them, and re-layouts: 3.86 us -> none  [apply_field(): returning = jnp.einsum('ks,kpi->spi', pair_f32, backward, precision=highest)]
    unnamed x10 -> x2, local copies, waits for them, and re-layouts: 0.03 us -> 2.95 us
    convert_element_type x3 -> x0, local copies, waits for them, and re-layouts: 2.43 us -> none  [the longest x2 1.76 us: apply_field(): outgoing = jnp.einsum('sc,cpi->spi', want_bf, field, preferred_element_ty...]
  transfers between devices with their start and end apart: 10 -> 0, of which waited for: 5 -> 0; matrix products, arithmetic and copies ran while one was open for 28% -> 0% of each run, Pallas kernels for 0% -> 0%
where the time goes in v1:
time: 24.5 us; the launch traced here: 24.3 us
  Pallas kernels  20.7 us (84%)
  local copies, waits for them, and re-layouts  2.95 us (12%)
  between operations  0.64 us (3%)
    pallas_call x1, Pallas kernels, per_device(): pl.pallas_call(functools.partial(kernel, slabs, peers, clusters, pairs, p...  20.7 us
    unnamed x2, local copies, waits for them, and re-layouts  2.95 us

profile of v1, /device:TPU:0, one launch (start us, length us, event | category | flops | bytes accessed | tf_op | source)
XLA Modules:
  0.0 24.3 jit_solution(15324984973055047643)
XLA Ops:
  0.6 20.7 %shard_map.77 = (f32[4,16,256]{2,1,0:T(8,128)}, f32[4,16,256]{2,1,0:T(8,128)}) custom-call(s32[24]{0:T(128)} %partner_ref.1, s32[24]{0:T(128)} %source_ref.1, f32[4,16,256]{2,1,0:T(8,128)} %phases_hbm.1, bf16[4,256,256]{2,1,0:T(8,128)(2,1)} %onsite_hbm.1, bf16[4,256,256]{2,1,0:T(8,128)(2,1)} %coupling_hbm.1, bf16[24,256,256]{2,1,0:T(8,128)(2,1)} %pairs_hbm.1), custom_call_target="tpu_custom_call" | custom-call | tf_op jit(solution)/shard_map/pallas_call | solution.py:251
  21.3 1.5 %copy.10 = f32[4,16,256]{2,1,0:T(8,128)} copy(f32[4,16,256]{2,1,0:T(8,128)} %get-tuple-element.4) | data formatting | bytes 131072
  22.8 1.5 %copy.11 = f32[4,16,256]{2,1,0:T(8,128)} copy(f32[4,16,256]{2,1,0:T(8,128)} %get-tuple-element.5) | data formatting | bytes 131072

commit v2 on v1

--- a/solution.py
+++ b/solution.py
@@ -41,9 +41,10 @@
     slabs, peers, clusters, pairs, probes, orb,
     partner_ref, source_ref, phases_hbm, onsite_hbm, coupling_hbm, pairs_hbm,
     first_ref, second_ref,
-    onsite, coupling, blocks, phases, start, fields_0, fields_1, own, above, going, coming, down_out, down_in,
+    onsite, coupling, blocks, phases, start, fields_0, fields_1, own, above, going, traded, leaving, coming, down_out, down_in,
     spread, collect, products_high, products_low,
-    load_sem, field_send, field_recv, prod_send, prod_recv, up_send, up_recv, down_send, down_recv,
+    load_sem, field_send, field_recv, hand_send, hand_recv, trade_send, trade_recv, prod_send, prod_recv,
+    up_send, up_recv, down_send, down_recv,
 ):
     slab = lax.axis_index("slab")
     me = lax.axis_index("xsec")
@@ -66,14 +67,26 @@
         load.start()
     phases_load, loads = loads[0], loads[1:]
 
+    chips = peers // 2
+    chip = me // 2
+    core = lax.rem(me, 2)
+    sibling = me + 1 - 2 * core
+
     def peer(offset):
-        return lax.rem(me + offset, peers)
-
+        return lax.rem(chip + offset, chips) * 2 + core
+
+    def origin(offset):
+        return lax.rem(chip - offset + chips, chips) * 2 + core
+
+    far = list(range(chips - 1, 0, -1))
     barrier = pltpu.get_barrier_semaphore()
-    for offset in range(1, peers):
+    for offset in far:
         pl.semaphore_signal(
             barrier, inc=1, device_id=(slab, peer(offset)), device_id_type=pl.DeviceIdType.MESH
         )
+    pl.semaphore_signal(
+        barrier, inc=1, device_id=(slab, sibling), device_id_type=pl.DeviceIdType.MESH
+    )
 
     @pl.when(slab > 0)
     def _():
@@ -104,20 +117,37 @@
     source_row = source_row * probes + inner
 
     neighbours = (slab > 0).astype(jnp.int32) + (slab < slabs - 1).astype(jnp.int32)
-    pl.semaphore_wait(barrier, peers - 1 + neighbours)
+    pl.semaphore_wait(barrier, chips + neighbours)
 
     def field_copy(step, offset):
         span = fields[step].at[pl.ds(me * clusters, clusters)]
         return pltpu.make_async_remote_copy(
             src_ref=span, dst_ref=span,
             send_sem=field_send.at[step, offset], recv_sem=field_recv.at[step, offset],
-            device_id=(slab, peer(offset)), device_id_type=pl.DeviceIdType.MESH,
+            device_id=(slab, peer(offset) if offset else sibling),
+            device_id_type=pl.DeviceIdType.MESH,
+        )
+
+    def handed_copy(step, offset):
+        span = fields[step].at[pl.ds(origin(offset) * clusters, clusters)]
+        return pltpu.make_async_remote_copy(
+            src_ref=span, dst_ref=span,
+            send_sem=hand_send.at[step, offset], recv_sem=hand_recv.at[step, offset],
+            device_id=(slab, sibling), device_id_type=pl.DeviceIdType.MESH,
+        )
+
+    def exchange_copy(step, offset):
+        target = lax.rem(chip + offset, chips) * 2 + 1 - core
+        return pltpu.make_async_remote_copy(
+            src_ref=going.at[step, pl.ds(target * rows, rows)],
+            dst_ref=traded.at[step, offset],
+            send_sem=trade_send.at[step, offset], recv_sem=trade_recv.at[step, offset],
+            device_id=(slab, sibling), device_id_type=pl.DeviceIdType.MESH,
         )
 
     def product_copy(step, offset):
         return pltpu.make_async_remote_copy(
-            src_ref=going.at[step, pl.ds(peer(offset) * rows, rows)],
-            dst_ref=coming.at[step, offset],
+            src_ref=leaving.at[step, offset], dst_ref=coming.at[step, offset],
             send_sem=prod_send.at[step, offset], recv_sem=prod_recv.at[step, offset],
             device_id=(slab, peer(offset)), device_id_type=pl.DeviceIdType.MESH,
         )
@@ -145,7 +175,7 @@
         field = value.astype(BF16).reshape(clusters, probes, orb)
         own[step] = field
         fields[step][pl.ds(me * clusters, clusters)] = field
-        for offset in range(1, peers):
+        for offset in far + [0]:
             field_copy(step, offset).start()
 
         @pl.when(slab > 0)
@@ -157,23 +187,24 @@
             spread[...] = (spread_rows == partner_row).astype(F32).astype(BF16)
             collect_rows = lax.broadcasted_iota(jnp.int32, collect.shape, 0)
             collect[...] = (collect_rows == source_row).astype(F32).astype(BF16)
-            loads[0].wait()
-        for c in range(clusters):
-            down_out[step, pl.ds(c * probes, probes)] = plain(field[c], coupling[c])
-
-        @pl.when(slab < slabs - 1)
-        def _():
-            down_copy(step).start()
-
         for k in range(pairs):
             if step == 0 and k % part == 0:
                 loads[1 + k // part].wait()
             keep(k, plain(own[step, source_ref[k]], blocks[k]))
         high = products_high[...]
         low = products_low[...]
-        going[step] = (plain(spread[...], high) + plain(spread[...], low)).astype(BF16)
-        for offset in range(1, peers):
-            product_copy(step, offset).start()
+        going[step] = plain(spread[...], high) + plain(spread[...], low)
+        for offset in far + [0]:
+            exchange_copy(step, offset).start()
+
+        if step == 0:
+            loads[0].wait()
+        for c in range(clusters):
+            down_out[step, pl.ds(c * probes, probes)] = plain(field[c], coupling[c])
+
+        @pl.when(slab < slabs - 1)
+        def _():
+            down_copy(step).start()
 
         if step == 0:
             loads[1 + CHUNKS].wait()
@@ -182,49 +213,62 @@
             local.append(0.5 * (plain(field[c], onsite[c]) + flipped(field[c], onsite[c])))
         result = jnp.concatenate(local, axis=0)
 
-        for offset in range(1, peers):
+        for offset in far:
+            exchange_copy(step, offset).wait_recv()
+            mine = going[step, pl.ds(peer(offset) * rows, rows)]
+            leaving[step, offset] = (mine + traded[step, offset]).astype(BF16)
+            product_copy(step, offset).start()
+        for offset in far[::-1]:
             field_copy(step, offset).wait_recv()
+            handed_copy(step, offset).start()
+        field_copy(step, 0).wait_recv()
+        exchange_copy(step, 0).wait_recv()
+        result = result + going[step, pl.ds(me * rows, rows)] + traded[step, 0]
+
+        @pl.when(slab < slabs - 1)
+        def _():
+            up_copy(step).wait_recv()
+
+        @pl.when(slab == slabs - 1)
+        def _():
+            above[step] = jnp.zeros_like(own[step])
+
+        result = result + jnp.concatenate(
+            [flipped(above[step, c], coupling[c]) for c in range(clusters)], axis=0
+        )
+
+        @pl.when(slab > 0)
+        def _():
+            down_copy(step).wait_recv()
+
+        @pl.when(slab == 0)
+        def _():
+            down_in[step] = jnp.zeros_like(start)
+
+        result = result + down_in[step]
+        for offset in far:
+            handed_copy(step, offset).wait_recv()
         for k in range(pairs):
             keep(k, flipped(fields[step][partner_ref[k]], blocks[k]))
         high = products_high[...]
         low = products_low[...]
         result = result + (plain(collect[...], high) + plain(collect[...], low))
-
-        @pl.when(slab < slabs - 1)
-        def _():
-            up_copy(step).wait_recv()
-
-        @pl.when(slab == slabs - 1)
-        def _():
-            above[step] = jnp.zeros_like(own[step])
-
-        result = result + jnp.concatenate(
-            [flipped(above[step, c], coupling[c]) for c in range(clusters)], axis=0
-        )
-
-        @pl.when(slab > 0)
-        def _():
-            down_copy(step).wait_recv()
-
-        @pl.when(slab == 0)
-        def _():
-            down_in[step] = jnp.zeros_like(start)
-
-        result = result + down_in[step]
-        result = result + going[step, pl.ds(me * rows, rows)].astype(F32)
-        for offset in range(1, peers):
+        for offset in far:
             product_copy(step, offset).wait_recv()
             result = result + coming[step, offset].astype(F32)
         return result * factor
 
     first = apply_field(0, begin)
-    first_ref[...] = first.reshape(clusters, probes, orb)
+    first_ref[...] = 0.5 * first.reshape(clusters, probes, orb)
     second = 2.0 * apply_field(1, first) - start[...]
-    second_ref[...] = second.reshape(clusters, probes, orb)
+    second_ref[...] = 0.5 * second.reshape(clusters, probes, orb)
 
     for step in range(2):
-        for offset in range(1, peers):
+        for offset in range(chips):
             field_copy(step, offset).wait_send()
+            exchange_copy(step, offset).wait_send()
+        for offset in far:
+            handed_copy(step, offset).wait_send()
             product_copy(step, offset).wait_send()
 
         @pl.when(slab > 0)
@@ -248,7 +292,7 @@
     hbm = pl.BlockSpec(memory_space=pltpu.HBM)
     dma = pltpu.SemaphoreType.DMA
     out = jax.ShapeDtypeStruct(phases.shape, F32)
-    return pl.pallas_call(
+    raw = pl.pallas_call(
         functools.partial(kernel, slabs, peers, clusters, pairs, probes, orb),
         out_shape=(out, out),
         in_specs=[smem, smem, hbm, hbm, hbm, hbm],
@@ -263,8 +307,10 @@
             pltpu.VMEM((slots, probes, orb), BF16),
             pltpu.VMEM((2, clusters, probes, orb), BF16),
             pltpu.VMEM((2, clusters, probes, orb), BF16),
-            pltpu.VMEM((2, slots * probes, orb), BF16),
-            pltpu.VMEM((2, peers, rows, orb), BF16),
+            pltpu.VMEM((2, slots * probes, orb), F32),
+            pltpu.VMEM((2, peers // 2, rows, orb), F32),
+            pltpu.VMEM((2, peers // 2, rows, orb), BF16),
+            pltpu.VMEM((2, peers // 2, rows, orb), BF16),
             pltpu.VMEM((2, rows, orb), F32),
             pltpu.VMEM((2, rows, orb), F32),
             pltpu.VMEM((slots * probes, pairs * probes), BF16),
@@ -272,13 +318,14 @@
             pltpu.VMEM((pairs * probes, orb), BF16),
             pltpu.VMEM((pairs * probes, orb), BF16),
             dma((3 + CHUNKS,)),
-            dma((2, peers)), dma((2, peers)), dma((2, peers)), dma((2, peers)),
+            *[dma((2, peers // 2)) for _ in range(8)],
             dma((2,)), dma((2,)), dma((2,)), dma((2,)),
         ],
         compiler_params=pltpu.CompilerParams(
             collective_id=0, has_side_effects=True, vmem_limit_bytes=63 * 1024 * 1024
         ),
     )(pair_partner, pair_source, phases, onsite, coupling, pair_blocks)
+    return 2.0 * raw[0], 2.0 * raw[1]
 
 
 def solution(mesh):

time: 24.5 us -> 20.5 us (0.84)
  local copies, waits for them, and re-layouts: 2.95 us -> 0 us
  Pallas kernels: 20.7 us -> 18.2 us
  other arithmetic: 0 us -> 1.53 us
    unnamed x2 -> x0, local copies, waits for them, and re-layouts: 2.95 us -> none
    pallas_call x1, Pallas kernels: 20.7 us -> 18.2 us  [per_device(): pl.pallas_call(functools.partial(kernel, slabs, peers, clusters, pairs, p...]
    mul x0 -> x1, other arithmetic: none -> 1.53 us  [per_device(): return (2.0 * raw[0], 2.0 * raw[1])]
where the time goes in v2:
time: 20.5 us; the launch traced here: 20.3 us
  Pallas kernels  18.2 us (89%)
  other arithmetic  1.53 us (7%)
  between operations  0.64 us (3%)
    pallas_call x1, Pallas kernels, per_device(): pl.pallas_call(functools.partial(kernel, slabs, peers, clusters, pairs, p...  18.2 us
    mul x1, other arithmetic, per_device(): return (2.0 * raw[0], 2.0 * raw[1])  1.53 us

profile of v2, /device:TPU:0, one launch (start us, length us, event | category | flops | bytes accessed | tf_op | source)
XLA Modules:
  0.0 20.3 jit_solution(12417405069154994716)
XLA Ops:
  0.6 18.2 %shard_map.77 = (f32[4,16,256]{2,1,0:T(8,128)}, f32[4,16,256]{2,1,0:T(8,128)}) custom-call(s32[24]{0:T(128)} %partner_ref.1, s32[24]{0:T(128)} %source_ref.1, f32[4,16,256]{2,1,0:T(8,128)} %phases_hbm.1, bf16[4,256,256]{2,1,0:T(8,128)(2,1)} %onsite_hbm.1, bf16[4,256,256]{2,1,0:T(8,128)(2,1)} %coupling_hbm.1, bf16[24,256,256]{2,1,0:T(8,128)(2,1)} %pairs_hbm.1), custom_call_target="tpu_custom_call" | custom-call | tf_op jit(solution)/shard_map/pallas_call | solution.py:295
  18.8 1.5 %broadcast_multiply_fusion = (f32[4,16,256]{2,1,0:T(8,128)}, f32[4,16,256]{2,1,0:T(8,128)}) fusion(f32[4,16,256]{2,1,0:T(8,128)} %get-tuple-element.5, f32[4,16,256]{2,1,0:T(8,128)} %get-tuple-element.4), kind=kLoop, calls=%fused_computation | loop fusion | flops 32768 | bytes 262144 | tf_op jit(solution)/shard_map/mul | solution.py:328

commit v3 on v2

--- a/solution.py
+++ b/solution.py
@@ -41,7 +41,7 @@
     slabs, peers, clusters, pairs, probes, orb,
     partner_ref, source_ref, phases_hbm, onsite_hbm, coupling_hbm, pairs_hbm,
     first_ref, second_ref,
-    onsite, coupling, blocks, phases, start, fields_0, fields_1, own, above, going, traded, leaving, coming, down_out, down_in,
+    onsite, coupling, blocks, phases, start, fields_0, fields_1, own, above, going, giving, traded, leaving, coming, down_out, down_in,
     spread, collect, products_high, products_low,
     load_sem, field_send, field_recv, hand_send, hand_recv, trade_send, trade_recv, prod_send, prod_recv,
     up_send, up_recv, down_send, down_recv,
@@ -105,6 +105,7 @@
     start[...] = begin
 
     width = pairs * probes
+    half = chips * rows
     lane = lax.broadcasted_iota(jnp.int32, (1, width), 1)
     group = lane // probes
     inner = lane % probes
@@ -113,11 +114,12 @@
     for k in range(pairs):
         partner_row = jnp.where(group == k, partner_ref[k], partner_row)
         source_row = jnp.where(group == k, source_ref[k], source_row)
+    device = partner_row // clusters
+    partner_row = (
+        lax.rem(device, 2) * (half // probes) + device // 2 * clusters + lax.rem(partner_row, clusters)
+    )
     partner_row = partner_row * probes + inner
     source_row = source_row * probes + inner
-
-    neighbours = (slab > 0).astype(jnp.int32) + (slab < slabs - 1).astype(jnp.int32)
-    pl.semaphore_wait(barrier, chips + neighbours)
 
     def field_copy(step, offset):
         span = fields[step].at[pl.ds(me * clusters, clusters)]
@@ -137,9 +139,9 @@
         )
 
     def exchange_copy(step, offset):
-        target = lax.rem(chip + offset, chips) * 2 + 1 - core
-        return pltpu.make_async_remote_copy(
-            src_ref=going.at[step, pl.ds(target * rows, rows)],
+        target = lax.rem(chip + offset, chips)
+        return pltpu.make_async_remote_copy(
+            src_ref=giving.at[step, pl.ds(target * rows, rows)],
             dst_ref=traded.at[step, offset],
             send_sem=trade_send.at[step, offset], recv_sem=trade_recv.at[step, offset],
             device_id=(slab, sibling), device_id_type=pl.DeviceIdType.MESH,
@@ -175,13 +177,28 @@
         field = value.astype(BF16).reshape(clusters, probes, orb)
         own[step] = field
         fields[step][pl.ds(me * clusters, clusters)] = field
-        for offset in far + [0]:
-            field_copy(step, offset).start()
-
-        @pl.when(slab > 0)
-        def _():
-            up_copy(step).start()
-
+
+        def send_fields():
+            for offset in far + [0]:
+                field_copy(step, offset).start()
+
+            @pl.when(slab > 0)
+            def _():
+                up_copy(step).start()
+
+        def send_down():
+            @pl.when(slab < slabs - 1)
+            def _():
+                down_copy(step).start()
+
+        def send_exchange():
+            for offset in far + [0]:
+                exchange_copy(step, offset).start()
+
+        if step == 0:
+            neighbours = (slab > 0).astype(jnp.int32) + (slab < slabs - 1).astype(jnp.int32)
+            pl.semaphore_wait(barrier, chips + neighbours)
+        send_fields()
         if step == 0:
             spread_rows = lax.broadcasted_iota(jnp.int32, spread.shape, 0)
             spread[...] = (spread_rows == partner_row).astype(F32).astype(BF16)
@@ -193,18 +210,16 @@
             keep(k, plain(own[step, source_ref[k]], blocks[k]))
         high = products_high[...]
         low = products_low[...]
-        going[step] = plain(spread[...], high) + plain(spread[...], low)
-        for offset in far + [0]:
-            exchange_copy(step, offset).start()
-
+        other = spread[pl.ds((1 - core) * half, half)]
+        giving[step] = (plain(other, high) + plain(other, low)).astype(BF16)
+        send_exchange()
         if step == 0:
             loads[0].wait()
         for c in range(clusters):
-            down_out[step, pl.ds(c * probes, probes)] = plain(field[c], coupling[c])
-
-        @pl.when(slab < slabs - 1)
-        def _():
-            down_copy(step).start()
+            down_out[step, pl.ds(c * probes, probes)] = plain(field[c], coupling[c]).astype(BF16)
+        send_down()
+        same = spread[pl.ds(core * half, half)]
+        going[step] = plain(same, high) + plain(same, low)
 
         if step == 0:
             loads[1 + CHUNKS].wait()
@@ -215,15 +230,15 @@
 
         for offset in far:
             exchange_copy(step, offset).wait_recv()
-            mine = going[step, pl.ds(peer(offset) * rows, rows)]
-            leaving[step, offset] = (mine + traded[step, offset]).astype(BF16)
+            mine = going[step, pl.ds(lax.rem(chip + offset, chips) * rows, rows)]
+            leaving[step, offset] = (mine + traded[step, offset].astype(F32)).astype(BF16)
             product_copy(step, offset).start()
         for offset in far[::-1]:
             field_copy(step, offset).wait_recv()
             handed_copy(step, offset).start()
         field_copy(step, 0).wait_recv()
         exchange_copy(step, 0).wait_recv()
-        result = result + going[step, pl.ds(me * rows, rows)] + traded[step, 0]
+        result = result + going[step, pl.ds(chip * rows, rows)] + traded[step, 0].astype(F32)
 
         @pl.when(slab < slabs - 1)
         def _():
@@ -243,9 +258,9 @@
 
         @pl.when(slab == 0)
         def _():
-            down_in[step] = jnp.zeros_like(start)
-
-        result = result + down_in[step]
+            down_in[step] = jnp.zeros(start.shape, BF16)
+
+        result = result + down_in[step].astype(F32)
         for offset in far:
             handed_copy(step, offset).wait_recv()
         for k in range(pairs):
@@ -307,12 +322,13 @@
             pltpu.VMEM((slots, probes, orb), BF16),
             pltpu.VMEM((2, clusters, probes, orb), BF16),
             pltpu.VMEM((2, clusters, probes, orb), BF16),
-            pltpu.VMEM((2, slots * probes, orb), F32),
-            pltpu.VMEM((2, peers // 2, rows, orb), F32),
+            pltpu.VMEM((2, slots * probes // 2, orb), F32),
+            pltpu.VMEM((2, slots * probes // 2, orb), BF16),
             pltpu.VMEM((2, peers // 2, rows, orb), BF16),
             pltpu.VMEM((2, peers // 2, rows, orb), BF16),
-            pltpu.VMEM((2, rows, orb), F32),
-            pltpu.VMEM((2, rows, orb), F32),
+            pltpu.VMEM((2, peers // 2, rows, orb), BF16),
+            pltpu.VMEM((2, rows, orb), BF16),
+            pltpu.VMEM((2, rows, orb), BF16),
             pltpu.VMEM((slots * probes, pairs * probes), BF16),
             pltpu.VMEM((rows, pairs * probes), BF16),
             pltpu.VMEM((pairs * probes, orb), BF16),

time: 20.5 us -> 20.1 us (0.980)
  Pallas kernels: 18.2 us -> 17.8 us
    pallas_call x1, Pallas kernels: 18.2 us -> 17.8 us  [per_device(): pl.pallas_call(functools.partial(kernel, slabs, peers, clusters, pairs, p...]
where the time goes in v3:
time: 20.1 us; the launch traced here: 19.9 us
  Pallas kernels  17.8 us (89%)
  other arithmetic  1.53 us (8%)
  between operations  0.64 us (3%)
    pallas_call x1, Pallas kernels, per_device(): pl.pallas_call(functools.partial(kernel, slabs, peers, clusters, pairs, p...  17.8 us
    mul x1, other arithmetic, per_device(): return (2.0 * raw[0], 2.0 * raw[1])  1.53 us

profile of v3, /device:TPU:0, one launch (start us, length us, event | category | flops | bytes accessed | tf_op | source)
XLA Modules:
  0.0 19.9 jit_solution(10655063622247325058)
XLA Ops:
  0.6 17.8 %shard_map.77 = (f32[4,16,256]{2,1,0:T(8,128)}, f32[4,16,256]{2,1,0:T(8,128)}) custom-call(s32[24]{0:T(128)} %partner_ref.1, s32[24]{0:T(128)} %source_ref.1, f32[4,16,256]{2,1,0:T(8,128)} %phases_hbm.1, bf16[4,256,256]{2,1,0:T(8,128)(2,1)} %onsite_hbm.1, bf16[4,256,256]{2,1,0:T(8,128)(2,1)} %coupling_hbm.1, bf16[24,256,256]{2,1,0:T(8,128)(2,1)} %pairs_hbm.1), custom_call_target="tpu_custom_call" | custom-call | tf_op jit(solution)/shard_map/pallas_call | solution.py:310
  18.4 1.5 %broadcast_multiply_fusion = (f32[4,16,256]{2,1,0:T(8,128)}, f32[4,16,256]{2,1,0:T(8,128)}) fusion(f32[4,16,256]{2,1,0:T(8,128)} %get-tuple-element.5, f32[4,16,256]{2,1,0:T(8,128)} %get-tuple-element.4), kind=kLoop, calls=%fused_computation | loop fusion | flops 32768 | bytes 262144 | tf_op jit(solution)/shard_map/mul | solution.py:344

commit v4 on v3

--- a/solution.py
+++ b/solution.py
@@ -63,9 +63,8 @@
             pltpu.make_async_copy(pairs_hbm.at[span], blocks.at[span], load_sem.at[1 + chunk])
         )
     loads.append(pltpu.make_async_copy(onsite_hbm, onsite, load_sem.at[1 + CHUNKS]))
-    for load in loads:
-        load.start()
     phases_load, loads = loads[0], loads[1:]
+    phases_load.start()
 
     chips = peers // 2
     chip = me // 2
@@ -100,27 +99,14 @@
             barrier, inc=1, device_id=(slab + 1, me), device_id_type=pl.DeviceIdType.MESH
         )
 
+    for load in loads:
+        load.start()
     phases_load.wait()
     begin = math.sqrt(2.0) * cosine(phases[...]).reshape(rows, orb)
     start[...] = begin
 
     width = pairs * probes
     half = chips * rows
-    lane = lax.broadcasted_iota(jnp.int32, (1, width), 1)
-    group = lane // probes
-    inner = lane % probes
-    partner_row = jnp.zeros((1, width), jnp.int32)
-    source_row = jnp.zeros((1, width), jnp.int32)
-    for k in range(pairs):
-        partner_row = jnp.where(group == k, partner_ref[k], partner_row)
-        source_row = jnp.where(group == k, source_ref[k], source_row)
-    device = partner_row // clusters
-    partner_row = (
-        lax.rem(device, 2) * (half // probes) + device // 2 * clusters + lax.rem(partner_row, clusters)
-    )
-    partner_row = partner_row * probes + inner
-    source_row = source_row * probes + inner
-
     def field_copy(step, offset):
         span = fields[step].at[pl.ds(me * clusters, clusters)]
         return pltpu.make_async_remote_copy(
@@ -200,6 +186,20 @@
             pl.semaphore_wait(barrier, chips + neighbours)
         send_fields()
         if step == 0:
+            lane = lax.broadcasted_iota(jnp.int32, (1, width), 1)
+            group = lane // probes
+            inner = lane % probes
+            partner_row = jnp.zeros((1, width), jnp.int32)
+            source_row = jnp.zeros((1, width), jnp.int32)
+            for k in range(pairs):
+                partner_row = jnp.where(group == k, partner_ref[k], partner_row)
+                source_row = jnp.where(group == k, source_ref[k], source_row)
+            device = partner_row // clusters
+            partner_row = (
+                lax.rem(device, 2) * (half // probes) + device // 2 * clusters + lax.rem(partner_row, clusters)
+            )
+            partner_row = partner_row * probes + inner
+            source_row = source_row * probes + inner
             spread_rows = lax.broadcasted_iota(jnp.int32, spread.shape, 0)
             spread[...] = (spread_rows == partner_row).astype(F32).astype(BF16)
             collect_rows = lax.broadcasted_iota(jnp.int32, collect.shape, 0)
@@ -221,13 +221,6 @@
         same = spread[pl.ds(core * half, half)]
         going[step] = plain(same, high) + plain(same, low)
 
-        if step == 0:
-            loads[1 + CHUNKS].wait()
-        local = []
-        for c in range(clusters):
-            local.append(0.5 * (plain(field[c], onsite[c]) + flipped(field[c], onsite[c])))
-        result = jnp.concatenate(local, axis=0)
-
         for offset in far:
             exchange_copy(step, offset).wait_recv()
             mine = going[step, pl.ds(lax.rem(chip + offset, chips) * rows, rows)]
@@ -236,6 +229,13 @@
         for offset in far[::-1]:
             field_copy(step, offset).wait_recv()
             handed_copy(step, offset).start()
+        if step == 0:
+            loads[1 + CHUNKS].wait()
+        local = []
+        for c in range(clusters):
+            local.append(0.5 * (plain(field[c], onsite[c]) + flipped(field[c], onsite[c])))
+        result = jnp.concatenate(local, axis=0)
+
         field_copy(step, 0).wait_recv()
         exchange_copy(step, 0).wait_recv()
         result = result + going[step, pl.ds(chip * rows, rows)] + traded[step, 0].astype(F32)

time: 20.1 us -> 19.9 us (0.990)
  Pallas kernels: 17.8 us -> 17.5 us
    pallas_call x1, Pallas kernels: 17.8 us -> 17.5 us  [per_device(): pl.pallas_call(functools.partial(kernel, slabs, peers, clusters, pairs, p...]
where the time goes in v4:
time: 19.9 us; the launch traced here: 19.7 us
  Pallas kernels  17.5 us (88%)
  other arithmetic  1.53 us (8%)
  between operations  0.64 us (3%)
    pallas_call x1, Pallas kernels, per_device(): pl.pallas_call(functools.partial(kernel, slabs, peers, clusters, pairs, p...  17.5 us
    mul x1, other arithmetic, per_device(): return (2.0 * raw[0], 2.0 * raw[1])  1.53 us

profile of v4, /device:TPU:0, one launch (start us, length us, event | category | flops | bytes accessed | tf_op | source)
XLA Modules:
  0.0 19.7 jit_solution(11008233844772074459)
XLA Ops:
  0.6 17.5 %shard_map.77 = (f32[4,16,256]{2,1,0:T(8,128)}, f32[4,16,256]{2,1,0:T(8,128)}) custom-call(s32[24]{0:T(128)} %partner_ref.1, s32[24]{0:T(128)} %source_ref.1, f32[4,16,256]{2,1,0:T(8,128)} %phases_hbm.1, bf16[4,256,256]{2,1,0:T(8,128)(2,1)} %onsite_hbm.1, bf16[4,256,256]{2,1,0:T(8,128)(2,1)} %coupling_hbm.1, bf16[24,256,256]{2,1,0:T(8,128)(2,1)} %pairs_hbm.1), custom_call_target="tpu_custom_call" | custom-call | tf_op jit(solution)/shard_map/pallas_call | solution.py:310
  18.2 1.5 %broadcast_multiply_fusion = (f32[4,16,256]{2,1,0:T(8,128)}, f32[4,16,256]{2,1,0:T(8,128)}) fusion(f32[4,16,256]{2,1,0:T(8,128)} %get-tuple-element.5, f32[4,16,256]{2,1,0:T(8,128)} %get-tuple-element.4), kind=kLoop, calls=%fused_computation | loop fusion | flops 32768 | bytes 262144 | tf_op jit(solution)/shard_map/mul | solution.py:344
